TPU v7x, 128 devices: a whole 4x4x4 slice. The times are simulated.
128 devices in a mesh: aux: 4 (over y_lo, core), pair: 32 (over z, y_hi, x).
Axes of the slice: x: 4, y: 4 (y_hi: 2, y_lo: 2; y = y_hi * 2 + y_lo), z: 4, core: 2. Of those that a mesh axis runs over, the one named last changes fastest.
Arguments:
- amplitudes: bfloat16 [65536, 512], P('pair', 'aux'), may hold values from -4 to 4
- coulomb: bfloat16 [65536, 512], P('pair'), may hold values from -12 to 12
- df_factors: bfloat16 [65536, 2048], P('pair', 'aux'), may hold values from -0.07861328 to 0.07861328
- thc_left: bfloat16 [512, 1536], P('pair', 'aux'), may hold values from -0.50390625 to 0.50390625
- thc_right: bfloat16 [512, 1536], P('pair', 'aux'), may hold values from -0.50390625 to 0.50390625
- occ_energy: float32 [128], P('pair'), may hold values from -2 to -0.5
- vir_energy: float32 [512], replicated, may hold values from 0.5 to 3
- pivot_energy: float32 [1], replicated, may hold values from -2 to -0.5
Outputs:
- updated: bfloat16 [65536, 512], P('pair', 'aux')
All inputs are finite; a program needn't handle non-finite values.
Results may differ from a plain program's by a relative error of at most 0.0051.
Values may be sent and summed in bfloat16 or wider, within the bound.
A program may use at most 64 MiB of HBM per device.

v0:
```python
import jax
import jax.numpy as jnp
from jax import lax
from jax.sharding import PartitionSpec as P

ITERS = 2


def per_device(
    amplitudes, coulomb, df_factors, thc_left, thc_right, occ_energy, vir_energy, pivot_energy
):
    column_index = lax.axis_index("aux")
    width = amplitudes.shape[1]
    rows = amplitudes.shape[0]
    nvirt = vir_energy.shape[0]
    nocc_local = rows // nvirt
    denom_full = (
        vir_energy[None, :, None]
        + vir_energy[None, None, :]
        - occ_energy[:, None, None]
        - pivot_energy[0]
    ).reshape(rows, nvirt)
    local = amplitudes
    whole = None
    for step in range(ITERS):
        whole = lax.all_gather(local, "aux", axis=1, tiled=True)
        left, right = (
            lax.all_gather(thc_left, "pair", axis=0, tiled=True),
            lax.all_gather(thc_right, "pair", axis=0, tiled=True),
        )
        gram = lax.dot_general(
            df_factors, whole, (((0,), (0,)), ((), ())), preferred_element_type=jnp.float32
        )
        gram = lax.psum(gram, "pair").astype(jnp.bfloat16)
        proj = jnp.dot(whole, right, preferred_element_type=jnp.float32).reshape(
            nocc_local, nvirt, right.shape[1]
        )
        middle = jnp.sum(proj * left.astype(jnp.float32)[None], axis=1)
        weighted = (
            (left.astype(jnp.float32)[None] * middle[:, None, :])
            .astype(jnp.bfloat16)
            .reshape(rows, right.shape[1])
        )
        ladder = lax.dot_general(
            weighted, right, (((1,), (1,)), ((), ())), preferred_element_type=jnp.float32
        )
        cycle = jnp.dot(df_factors, gram, preferred_element_type=jnp.float32)
        part = cycle + ladder
        share = lax.psum_scatter(part, "aux", scatter_dimension=1, tiled=True)
        coulomb_block = lax.dynamic_slice_in_dim(coulomb, column_index * width, width, 1)
        denom_block = lax.dynamic_slice_in_dim(denom_full, column_index * width, width, 1)
        local = ((coulomb_block.astype(jnp.float32) + share) / denom_block).astype(jnp.bfloat16)
        whole = None
    return local


def solution(mesh):
    in_specs = (
        P("pair", "aux"),
        P("pair", None),
        P("pair", "aux"),
        P("pair", "aux"),
        P("pair", "aux"),
        P("pair"),
        P(),
        P(),
    )
    out_specs = P("pair", "aux")
    return jax.shard_map(
        per_device, mesh=mesh, in_specs=in_specs, out_specs=out_specs, check_vma=False
    )
```

profile of v0, /device:TPU:1, one launch (start us, length us, event | category | flops | bytes accessed | tf_op | source)
XLA Modules:
  0.0 727.8 jit_solution(6331696356727031182)
XLA Ops:
  6.5 0.0 copy-start
  6.5 0.0 all-gather.3.cloned.1.call-start
  6.5 0.7 all-gather.3.cloned.1.call-update
  7.3 0.0 reduce-scatter.3.cloned.1.call-start
  7.3 85.5 %all_gather.15 = bf16[512,384]{1,0:T(8,128)(2,1)S(1)} all-gather(bf16[16,384]{1,0:T(8,128)(2,1)} %param.11), channel_id=1, replica_groups=mesh['aux'=4,'pair'=32] {'pair'}, dimensions={0}, use_global_device_ids=true | all-gather | bytes 405504 | tf_op jit(solution)/shard_map/all_gather | solution.py:28
  92.8 0.1 convert_element_type.38
  92.9 0.0 copy-done.6
  92.9 75.5 %all_gather.16 = bf16[512,384]{1,0:T(8,128)(2,1)S(1)} all-gather(bf16[16,384]{1,0:T(8,128)(2,1)S(1)} %copy-done.6), channel_id=1, replica_groups=mesh['aux'=4,'pair'=32] {'pair'}, dimensions={0}, use_global_device_ids=true | all-gather | bytes 405504 | tf_op jit(solution)/shard_map/all_gather | solution.py:29
  168.3 3.0 multiply_reduce_fusion.1
  171.3 1.5 multiply_convert_fusion.1
  172.8 0.0 copy-done
  172.8 0.0 copy-done.4
  172.8 2.3 fusion.9
  175.1 162.7 %all-reduce.2 = bf16[512,512]{1,0:T(8,128)(2,1)} all-reduce(f32[512,512]{1,0:T(8,128)} %fusion.9), channel_id=1, replica_groups=mesh['aux'=4,'pair'=32] {'pair'}, use_global_device_ids=true, to_apply=%region_0.0 | all-reduce | flops 262144 | bytes 1572864 | tf_op jit(solution)/shard_map/psum | solution.py:34
  337.7 2.5 fusion.11
  340.2 0.0 copy-done.2
  340.2 3.3 bitcast_add_fusion.1
  343.5 0.0 reduce-scatter.3.cloned.1.call-update
  343.6 0.0 copy-start.7
  343.6 0.0 all-gather.5.cloned.1.call-start
  343.6 1.9 constant_dynamic-slice_fusion
  345.5 2.0 copy.15
  347.5 0.0 copy-done.7
  347.5 0.1 broadcast_add_fusion
  347.7 0.7 sub.27
  348.4 0.0 copy-start.8
  348.4 3.9 copy.17
  352.3 0.0 copy-done.8
  352.3 0.1 broadcast_bitcast_fusion
  353.0 86.1 %reduce-scatter.3.cloned.1.call-done = f32[2048,128]{0,1:T(8,128)} async-done(((f32[2048,512]{0,1:T(8,128)}), f32[2048,128]{0,1:T(8,128)}) %reduce-scatter.3.cloned.1.call-update) | async-done | bytes 1048592 | tf_op jit(solution)/shard_map/reduce_scatter | solution.py:49
  439.1 2.7 fusion.1
  441.9 0.0 all-gather.5.cloned.1.call-update
  441.9 0.0 reduce-scatter.5.cloned.1.call-start
  441.9 30.3 %all-gather.5.cloned.1.call-done = bf16[2048,512]{0,1:T(8,128)(2,1)} async-done(((bf16[2048,128]{0,1:T(8,128)(2,1)}), bf16[2048,512]{0,1:T(8,128)(2,1)}) %all-gather.5.cloned.1.call-update) | async-done | bytes 2097168 | tf_op jit(solution)/shard_map/all_gather | solution.py:26
  472.2 3.0 multiply_reduce_fusion
  475.3 1.5 multiply_convert_fusion
  476.7 0.0 copy-done.5
  476.7 2.2 convolution_bitcast_fusion
  479.0 168.0 %all-reduce.3 = bf16[512,512]{0,1:T(8,128)(2,1)S(1)} all-reduce(f32[512,512]{0,1:T(8,128)} %convolution_bitcast_fusion), channel_id=1, replica_groups=mesh['aux'=4,'pair'=32] {'pair'}, use_global_device_ids=true, to_apply=%region_3.0 | all-reduce | flops 262144 | bytes 1572864 | tf_op jit(solution)/shard_map/psum | solution.py:34
  647.0 0.0 copy-start.1
  647.0 1.3 fusion.10
  648.3 0.1 copy-done.1
  648.4 3.3 bitcast_add_fusion
  651.8 0.0 reduce-scatter.5.cloned.1.call-update
  651.8 66.7 %reduce-scatter.5.cloned.1.call-done = f32[2048,128]{0,1:T(8,128)} async-done(((f32[2048,512]{0,1:T(8,128)}), f32[2048,128]{0,1:T(8,128)}) %reduce-scatter.5.cloned.1.call-update) | async-done | bytes 1048592 | tf_op jit(solution)/shard_map/reduce_scatter | solution.py:49
  718.5 0.0 copy-done.3
  718.5 1.8 fusion.3
  720.3 1.0 copy.12
  (7 shorter events, 0.0 us)
Async XLA Ops:
  6.5 166.3 %copy-start = (bf16[2048,512]{1,0:T(8,128)(2,1)S(1)}, bf16[2048,512]{1,0:T(8,128)(2,1)}, u32[]{:S(2)}) copy-start(bf16[2048,512]{1,0:T(8,128)(2,1)} %param.10) | copy-start | bytes 6291460
  6.5 86.3 %copy-start.6 = (bf16[16,384]{1,0:T(8,128)(2,1)S(1)}, bf16[16,384]{1,0:T(8,128)(2,1)}, u32[]{:S(2)}) copy-start(bf16[16,384]{1,0:T(8,128)(2,1)} %param.12) | copy-start | bytes 36868
  6.5 161.8 %all-gather.3.cloned.1.call-start = ((), (), s32[]{:S(2)}) async-start(), calls=%async_computation.2 | async-start | bytes 2621440 | tf_op jit(solution)/shard_map/all_gather | solution.py:26
  7.3 431.9 %reduce-scatter.3.cloned.1.call-start = ((), (), s32[]{:S(2)}) async-start(), calls=%async_computation.3 | async-start | bytes 5242880 | tf_op jit(solution)/shard_map/reduce_scatter | solution.py:49
  168.3 4.5 copy-start.4
  337.7 2.5 copy-start.2
  343.6 4.0 copy-start.7
  343.6 128.6 %all-gather.5.cloned.1.call-start = ((), (), s32[]{:S(2)}) async-start(), calls=%async_computation.4 | async-start | bytes 2621440 | tf_op jit(solution)/shard_map/all_gather | solution.py:26
  348.4 3.9 copy-start.8
  441.9 276.6 %reduce-scatter.5.cloned.1.call-start = ((), (), s32[]{:S(2)}) async-start(), calls=%async_computation.5 | async-start | bytes 5242880 | tf_op jit(solution)/shard_map/reduce_scatter | solution.py:49
  472.2 4.5 copy-start.5
  647.0 1.4 copy-start.1
  651.8 66.7 %copy-start.3 = (bf16[2048,128]{0,1:T(8,128)(2,1)S(1)}, bf16[2048,128]{0,1:T(8,128)(2,1)}, u32[]{:S(2)}) copy-start(bf16[2048,128]{0,1:T(8,128)(2,1)} %copy.15) | copy-start | bytes 1572868
Sparse Core Ops, SparseCore 0:
  9.0 33.8 all-gather.2
  343.7 95.4 reduce-scatter.2
  442.0 30.1 all-gather.4
  651.9 66.5 reduce-scatter.4
where the time goes:
time: 728 us
  blocking collectives  492 us (68%)
  waiting for transfers between devices  184 us (25%)
  matrix products  20.9 us (3%)
  between operations  13.9 us (2%)
  local copies, waits for them, and re-layouts  9.74 us (1%)
  other arithmetic  7.65 us (1%)
    psum x2, blocking collectives, per_device(): gram = lax.psum(gram, 'pair').astype(jnp.bfloat16)  331 us
    reduce_scatter x2, waiting for transfers between devices, per_device(): share = lax.psum_scatter(part, 'aux', scatter_dimension=1, tiled=True)  153 us
    all_gather x1, blocking collectives, per_device(): lax.all_gather(thc_left, 'pair', axis=0, tiled=True)  85.5 us
    all_gather x1, blocking collectives, per_device(): lax.all_gather(thc_right, 'pair', axis=0, tiled=True)  75.5 us
    all_gather x2, waiting for transfers between devices, per_device(): whole = lax.all_gather(local, 'aux', axis=1, tiled=True)  30.3 us
  transfers between devices with their start and end apart: 4, of which 3 were waited for; matrix products, arithmetic and copies ran while one was open for 1% of the time, Pallas kernels for 0%

commit v1 on v0

--- a/solution.py
+++ b/solution.py
@@ -4,6 +4,11 @@
 from jax.sharding import PartitionSpec as P
 
 ITERS = 2
+
+
+def exchange_gather(x, axis, dim):
+    outgoing = jnp.stack([x] * lax.axis_size(axis))
+    return jnp.concatenate(lax.all_to_all(outgoing, axis, 0, 0), axis=dim)
 
 
 def per_device(
@@ -26,7 +31,7 @@
         whole = lax.all_gather(local, "aux", axis=1, tiled=True)
         left, right = (
             lax.all_gather(thc_left, "pair", axis=0, tiled=True),
-            lax.all_gather(thc_right, "pair", axis=0, tiled=True),
+            exchange_gather(thc_right, "pair", 0),
         )
         gram = lax.dot_general(
             df_factors, whole, (((0,), (0,)), ((), ())), preferred_element_type=jnp.float32

time: 728 us -> 656 us (0.901)
  blocking collectives: 492 us -> 413 us
  waiting for transfers between devices: 184 us -> 171 us
  starting transfers between devices: 0.12 us -> 11.5 us
    all_gather x1 -> x0, blocking collectives: 75.5 us -> none  [per_device(): lax.all_gather(thc_right, 'pair', axis=0, tiled=True)]
    reduce_scatter x2, waiting for transfers between devices: 153 us -> 140 us  [per_device(): share = lax.psum_scatter(part, 'aux', scatter_dimension=1, tiled=True)]
    all_to_all x0 -> x1, starting transfers between devices: none -> 11.3 us  [exchange_gather(): return jnp.concatenate(lax.all_to_all(outgoing, axis, 0, 0), axis=dim)]
  transfers between devices with their start and end apart: 4 -> 5, of which waited for: 3 -> 3; matrix products, arithmetic and copies ran while one was open for 1% -> 1% of each run, Pallas kernels for 0% -> 0%
where the time goes in v1:
time: 656 us; the launch traced here: 655 us
  blocking collectives  413 us (63%)
  waiting for transfers between devices  171 us (26%)
  matrix products  21.9 us (3%)
  local copies, waits for them, and re-layouts  15.6 us (2%)
  between operations  14 us (2%)
  starting transfers between devices  11.5 us (2%)
  other arithmetic  7.51 us (1%)
    psum x2, blocking collectives, per_device(): gram = lax.psum(gram, 'pair').astype(jnp.bfloat16)  330 us
    reduce_scatter x2, waiting for transfers between devices, per_device(): share = lax.psum_scatter(part, 'aux', scatter_dimension=1, tiled=True)  140 us
    all_gather x1, blocking collectives, per_device(): lax.all_gather(thc_left, 'pair', axis=0, tiled=True)  83.4 us
    all_gather x2, waiting for transfers between devices, per_device(): whole = lax.all_gather(local, 'aux', axis=1, tiled=True)  30.3 us
  transfers between devices with their start and end apart: 5, of which 3 were waited for; matrix products, arithmetic and copies ran while one was open for 1% of the time, Pallas kernels for 0%

profile of v1, /device:TPU:1, one launch (start us, length us, event | category | flops | bytes accessed | tf_op | source)
XLA Modules:
  0.0 654.8 jit_solution(6842556269151338896)
XLA Ops:
  6.5 0.0 copy-start
  6.5 0.0 all-gather.3.cloned.1.call-start
  6.5 0.7 all-gather.3.cloned.1.call-update
  7.3 1.5 stack.2
  8.7 11.3 %all-to-all-start = ((bf16[32,16,384]{2,1,0:T(8,128)(2,1)}), bf16[32,16,384]{2,1,0:T(8,128)(2,1)S(1)}, u32[]{:S(2)}, u32[]{:S(2)}) async-start(bf16[32,16,384]{2,1,0:T(8,128)(2,1)} %stack.2), calls=%async_computation | async-start | bytes 786432 | tf_op jit(solution)/shard_map/all_to_all | solution.py:11
  20.1 0.0 reduce-scatter.3.cloned.1.call-start
  20.1 83.4 %all_gather.11 = bf16[512,384]{1,0:T(8,128)(2,1)S(1)} all-gather(bf16[16,384]{1,0:T(8,128)(2,1)} %param.11), channel_id=1, replica_groups=mesh['aux'=4,'pair'=32] {'pair'}, dimensions={0}, use_global_device_ids=true | all-gather | bytes 405504 | tf_op jit(solution)/shard_map/all_gather | solution.py:33
  103.6 0.1 convert_element_type.50
  103.6 0.0 all-to-all-done
  103.7 0.0 all-gather.3.cloned.1.call-done
  103.7 3.0 multiply_reduce_fusion.1
  106.7 1.5 multiply_convert_fusion.1
  108.2 0.0 copy-done
  108.2 0.7 copy-done.8
  108.8 2.3 fusion.9
  111.1 161.1 %all-reduce.2 = bf16[512,512]{1,0:T(8,128)(2,1)} all-reduce(f32[512,512]{1,0:T(8,128)} %fusion.9), channel_id=1, replica_groups=mesh['aux'=4,'pair'=32] {'pair'}, use_global_device_ids=true, to_apply=%region_0.0 | all-reduce | flops 262144 | bytes 1572864 | tf_op jit(solution)/shard_map/psum | solution.py:39
  272.2 2.5 fusion.11
  274.6 3.3 bitcast_add_fusion.1
  278.0 0.0 reduce-scatter.3.cloned.1.call-update
  278.0 0.0 copy-start.6
  278.0 0.0 all-gather.5.cloned.1.call-start
  278.1 1.9 constant_dynamic-slice_fusion
  279.9 1.2 copy.17
  281.2 0.1 broadcast_add_fusion
  281.3 0.7 sub.27
  282.1 0.0 copy-start.7
  282.1 3.9 copy.19
  286.0 0.0 copy-done.7
  286.0 0.1 broadcast_bitcast_fusion
  286.7 73.5 %reduce-scatter.3.cloned.1.call-done = f32[2048,128]{0,1:T(8,128)} async-done(((f32[2048,512]{0,1:T(8,128)}), f32[2048,128]{0,1:T(8,128)}) %reduce-scatter.3.cloned.1.call-update) | async-done | bytes 1048592 | tf_op jit(solution)/shard_map/reduce_scatter | solution.py:54
  360.2 2.6 fusion.1
  362.8 0.0 all-gather.5.cloned.1.call-update
  362.8 0.0 reduce-scatter.5.cloned.1.call-start
  362.8 30.3 %all-gather.5.cloned.1.call-done = bf16[2048,512]{0,1:T(8,128)(2,1)} async-done(((bf16[2048,128]{0,1:T(8,128)(2,1)}), bf16[2048,512]{0,1:T(8,128)(2,1)}) %all-gather.5.cloned.1.call-update) | async-done | bytes 2097168 | tf_op jit(solution)/shard_map/all_gather | solution.py:31
  393.1 4.0 copy.16
  397.0 2.9 multiply_reduce_fusion
  399.9 1.5 multiply_convert_fusion
  401.4 0.7 copy-done.5
  402.1 2.2 convolution_bitcast_fusion
  404.3 168.6 %all-reduce.3 = bf16[512,512]{0,1:T(8,128)(2,1)} all-reduce(f32[512,512]{0,1:T(8,128)} %convolution_bitcast_fusion), channel_id=1, replica_groups=mesh['aux'=4,'pair'=32] {'pair'}, use_global_device_ids=true, to_apply=%region_3.0 | all-reduce | flops 262144 | bytes 1572864 | tf_op jit(solution)/shard_map/psum | solution.py:39
  572.9 2.5 fusion.10
  575.4 0.0 copy-done.1
  575.4 0.0 copy-done.4
  575.4 3.3 bitcast_add_fusion
  578.7 0.0 reduce-scatter.5.cloned.1.call-update
  578.8 66.7 %reduce-scatter.5.cloned.1.call-done = f32[2048,128]{0,1:T(8,128)} async-done(((f32[2048,512]{0,1:T(8,128)}), f32[2048,128]{0,1:T(8,128)}) %reduce-scatter.5.cloned.1.call-update) | async-done | bytes 1048592 | tf_op jit(solution)/shard_map/reduce_scatter | solution.py:54
  645.5 1.8 fusion.3
  647.3 1.0 copy.13
  (10 shorter events, 0.0 us)
Async XLA Ops:
  6.5 101.6 %copy-start = (bf16[2048,512]{1,0:T(8,128)(2,1)S(1)}, bf16[2048,512]{1,0:T(8,128)(2,1)}, u32[]{:S(2)}) copy-start(bf16[2048,512]{1,0:T(8,128)(2,1)} %param.10) | copy-start | bytes 6291460
  6.5 97.1 %all-gather.3.cloned.1.call-start = ((), (), s32[]{:S(2)}) async-start(), calls=%async_computation.3 | async-start | bytes 2621440 | tf_op jit(solution)/shard_map/all_gather | solution.py:31
  8.7 94.9 %all-to-all-start = ((bf16[32,16,384]{2,1,0:T(8,128)(2,1)}), bf16[32,16,384]{2,1,0:T(8,128)(2,1)S(1)}, u32[]{:S(2)}, u32[]{:S(2)}) async-start(bf16[32,16,384]{2,1,0:T(8,128)(2,1)} %stack.2), calls=%async_computation | async-start | bytes 786432 | tf_op jit(solution)/shard_map/all_to_all | solution.py:11
  20.1 340.1 %reduce-scatter.3.cloned.1.call-start = ((), (), s32[]{:S(2)}) async-start(), calls=%async_computation.4 | async-start | bytes 5242880 | tf_op jit(solution)/shard_map/reduce_scatter | solution.py:54
  103.6 171.0 %copy-start.3 = (bf16[32,16,384]{2,1,0:T(8,128)(2,1)}, bf16[32,16,384]{2,1,0:T(8,128)(2,1)S(1)}, u32[]{:S(2)}) copy-start(bf16[32,16,384]{2,1,0:T(8,128)(2,1)S(1)} %all-to-all-done) | copy-start | bytes 1179652
  106.7 2.2 copy-start.8
  272.2 2.5 copy-start.2
  278.0 3.2 copy-start.6
  278.0 115.1 %all-gather.5.cloned.1.call-start = ((), (), s32[]{:S(2)}) async-start(), calls=%async_computation.5 | async-start | bytes 2621440 | tf_op jit(solution)/shard_map/all_gather | solution.py:31
  282.1 3.9 copy-start.7
  362.8 282.7 %reduce-scatter.5.cloned.1.call-start = ((), (), s32[]{:S(2)}) async-start(), calls=%async_computation.6 | async-start | bytes 5242880 | tf_op jit(solution)/shard_map/reduce_scatter | solution.py:54
  399.9 2.2 copy-start.5
  572.9 2.5 copy-start.1
  572.9 2.5 copy-start.4
Sparse Core Ops, SparseCore 0:
  9.0 35.9 all-gather.2
  278.1 82.0 reduce-scatter.2
  362.9 30.1 all-gather.4
  578.9 66.5 reduce-scatter.4
